TPU v7x, 128 devices: a whole 4x4x4 slice. The times are simulated.
128 devices in a mesh: thinker: 4 (over z), seq: 32 (over y, x, core).
Axes of the slice: x: 4, y: 4, z: 4, core: 2. Of those that a mesh axis runs over, the one named last changes fastest.
Arguments:
- queries: bfloat16 [4, 4096, 2048], P('thinker', 'seq'), may hold values from -6 to 6
- keys: bfloat16 [4, 4096, 512], P('thinker', 'seq'), may hold values from -6 to 6
- values: bfloat16 [4, 4096, 512], P('thinker', 'seq'), may hold values from -6 to 6
- forward_out: bfloat16 [4, 4096, 2048], P('thinker', 'seq'), may hold values from -2 to 2
- logsumexp: float32 [4, 16, 4096], P('thinker', None, 'seq'), may hold values from -1 to 16, as said below
- upstream: bfloat16 [128, 128, 2048], P(None, ('thinker', 'seq')), may hold values from -6 to 6
- lengths: int32 [4], replicated, may hold values from 512 to 4096, as said below
- sibling_mask: int32 [4, 3, 32], P('thinker', None, 'seq'), may hold values from 0 to 1, as said below
Outputs:
- query_grad: bfloat16 [4, 4096, 2048], P('thinker', 'seq')
- key_grad: bfloat16 [4, 4096, 512], P('thinker', 'seq')
- value_grad: bfloat16 [4, 4096, 512], P('thinker', 'seq')
Inputs may be any that keep to these rules, and one draw needn't show every extreme that they name: lengths[t] valid positions stand at the start of thinker t's trace; two thinkers have exactly 4096, one exactly 512. sibling_mask[t, r, b] = 1 where query block b of thinker t reads the recent tokens of thinker (t + r + 1) % 4; the two thinkers of length 4096 read each other in the blocks of the last 128 positions. `logsumexp`: rows of positions past a trace's length carry arbitrary values.
All inputs are finite; a program needn't handle non-finite values.
Results may differ from a plain program's by a relative error of at most 0.014.
Values may be sent and summed in bfloat16 or wider, within the bound.
No kernel may reach another device: no remote copies, remote signals or barrier semaphores. Data moves between devices by JAX's collectives and lax.ppermute only.
A program may use at most 128 MiB of HBM per device.

v0:
```python
import math
import jax
import jax.numpy as jnp
from jax import lax
from jax.sharding import PartitionSpec as P

BLOCK = 128


def from_behind(block, axis, distance):
    devices = range(lax.axis_size(axis))
    route = [(i - distance, i) for i in devices if i - distance in devices]
    return lax.ppermute(block, axis, route)


def pair_grads(
    query_heads, upstream_heads, lse_heads, delta_heads, key_rows, value_rows, allowed, factor
):
    count = key_rows.shape[0]
    kv_heads = query_heads.shape[1]
    head_dim = query_heads.shape[3]
    key_heads = key_rows.reshape(count, kv_heads, head_dim)
    value_heads = value_rows.reshape(count, kv_heads, head_dim)
    scores = (
        jnp.einsum("ikgd,jkd->kgij", query_heads, key_heads, preferred_element_type=jnp.float32)
        * factor
    )
    probs = jnp.where(allowed, jnp.exp(scores - lse_heads[..., None]), 0.0)
    dprobs = jnp.einsum(
        "ikgd,jkd->kgij", upstream_heads, value_heads, preferred_element_type=jnp.float32
    )
    dscores = probs * (dprobs - delta_heads[..., None])
    probs_low = probs.astype(jnp.bfloat16)
    dscores_low = dscores.astype(jnp.bfloat16)
    value_part = jnp.einsum(
        "kgij,ikgd->jkd", probs_low, upstream_heads, preferred_element_type=jnp.float32
    )
    key_part = (
        jnp.einsum("kgij,ikgd->jkd", dscores_low, query_heads, preferred_element_type=jnp.float32)
        * factor
    )
    query_part = (
        jnp.einsum("kgij,jkd->ikgd", dscores_low, key_heads, preferred_element_type=jnp.float32)
        * factor
    )
    rows = query_heads.shape[0]
    return (
        query_part.reshape(rows, -1),
        key_part.reshape(count, -1),
        value_part.reshape(count, -1),
    )


def shards(queries, keys, values, forward_out, logsumexp, upstream, lengths, sibling_mask):
    thinkers = lax.axis_size("thinker")
    seq_count = lax.axis_size("seq")
    devices = thinkers * seq_count
    rows = queries.shape[1]
    qwidth = queries.shape[2]
    kwidth = keys.shape[2]
    heads = logsumexp.shape[1]
    head_dim = qwidth // heads
    kv_heads = kwidth // head_dim
    group = heads // kv_heads
    factor = head_dim ** (-0.5)
    thinker = lax.axis_index("thinker")
    shard = lax.axis_index("seq")
    length = rows * seq_count
    per_peer = rows // devices
    arranged = upstream.reshape(devices, per_peer, 1, qwidth)
    arrived = lax.all_to_all(arranged, ("thinker", "seq"), split_axis=0, concat_axis=2, tiled=True)
    grad_out = arrived.reshape(rows, qwidth)
    query_heads = queries[0].reshape(rows, kv_heads, group, head_dim)
    upstream_heads = grad_out.reshape(rows, kv_heads, group, head_dim)
    output_heads = forward_out[0].reshape(rows, kv_heads, group, head_dim)
    delta = jnp.sum(upstream_heads.astype(jnp.float32) * output_heads.astype(jnp.float32), axis=-1)
    delta_heads = jnp.transpose(delta, (1, 2, 0))
    lse_heads = logsumexp[0].reshape(kv_heads, group, rows)
    my_length = lengths[thinker]
    first_query = shard * rows
    query_pos = first_query + jnp.arange(rows, dtype=jnp.int32)
    query_live = query_pos < my_length

    def own_block(key_rows, value_rows, key_start):
        count = key_rows.shape[0]
        key_pos = key_start + jnp.arange(count, dtype=jnp.int32)
        allowed = (
            (key_pos[None, :] <= query_pos[:, None])
            & query_live[:, None]
            & (key_pos[None, :] < my_length)
        )
        return pair_grads(
            query_heads,
            upstream_heads,
            lse_heads,
            delta_heads,
            key_rows,
            value_rows,
            allowed,
            factor,
        )

    initial = (
        jnp.zeros((rows, qwidth), jnp.float32),
        jnp.zeros((length, kwidth), jnp.bfloat16),
        jnp.zeros((length, kwidth), jnp.bfloat16),
    )
    piece_keys = lax.all_gather(keys, "seq", axis=1, tiled=True)[0]
    piece_values = lax.all_gather(values, "seq", axis=1, tiled=True)[0]
    piece_rows = piece_keys.shape[0]
    sub_rows = math.gcd(piece_rows, 512)

    def one_block(position, inner):
        total, key_buffer, value_buffer = inner
        offset = position * sub_rows
        key_rows = lax.dynamic_slice_in_dim(piece_keys, offset, sub_rows, 0)
        value_rows = lax.dynamic_slice_in_dim(piece_values, offset, sub_rows, 0)
        query_part, key_part, value_part = own_block(key_rows, value_rows, offset)
        key_buffer = lax.dynamic_update_slice_in_dim(
            key_buffer, key_part.astype(jnp.bfloat16), offset, 0
        )
        value_buffer = lax.dynamic_update_slice_in_dim(
            value_buffer, value_part.astype(jnp.bfloat16), offset, 0
        )
        return (total + query_part, key_buffer, value_buffer)

    query_total, key_buffer, value_buffer = lax.fori_loop(
        0, piece_rows // sub_rows, one_block, initial
    )
    own_key, own_value = (
        lax.psum_scatter(key_buffer, "seq", scatter_dimension=0, tiled=True).astype(jnp.float32),
        lax.psum_scatter(value_buffer, "seq", scatter_dimension=0, tiled=True).astype(jnp.float32),
    )
    sibling_keys, sibling_values = (
        lax.all_gather(keys, "thinker", axis=0, tiled=True),
        lax.all_gather(values, "thinker", axis=0, tiled=True),
    )
    prior_keys, prior_values = from_behind((sibling_keys, sibling_values), "seq", 1)
    window_keys = jnp.roll(jnp.concatenate([prior_keys, sibling_keys], axis=1), -thinker, axis=0)
    window_values = jnp.roll(
        jnp.concatenate([prior_values, sibling_values], axis=1), -thinker, axis=0
    )
    key_pos = first_query - rows + jnp.arange(2 * rows, dtype=jnp.int32)
    near = (
        (key_pos[None, :] <= query_pos[:, None])
        & (key_pos[None, :] > query_pos[:, None] - rows)
        & (key_pos[None, :] >= 0)
        & query_live[:, None]
    )
    mask_rows = sibling_mask[0]
    key_terms_list = [jnp.zeros((2 * rows, kwidth), jnp.float32)]
    value_terms_list = [jnp.zeros((2 * rows, kwidth), jnp.float32)]
    for offset in range(1, thinkers):
        sibling = (thinker + offset) % thinkers
        visible = jnp.repeat(mask_rows[offset - 1], BLOCK) == 1
        allowed = near & visible[:, None] & (key_pos[None, :] < lengths[sibling])
        extra_query, extra_key, extra_value = pair_grads(
            query_heads,
            upstream_heads,
            lse_heads,
            delta_heads,
            window_keys[offset],
            window_values[offset],
            allowed,
            factor,
        )
        query_total = query_total + extra_query
        key_terms_list.append(extra_key)
        value_terms_list.append(extra_value)
    key_stack = jnp.roll(jnp.stack(key_terms_list), thinker, axis=0)
    value_stack = jnp.roll(jnp.stack(value_terms_list), thinker, axis=0)
    sibling_key, sibling_value = (
        lax.psum_scatter(
            key_stack.astype(jnp.bfloat16), "thinker", scatter_dimension=0, tiled=True
        ).astype(jnp.float32),
        lax.psum_scatter(
            value_stack.astype(jnp.bfloat16), "thinker", scatter_dimension=0, tiled=True
        ).astype(jnp.float32),
    )
    earlier_key, earlier_value = (
        from_behind(sibling_key[0, :rows].astype(jnp.bfloat16), "seq", -1).astype(jnp.float32),
        from_behind(sibling_value[0, :rows].astype(jnp.bfloat16), "seq", -1).astype(jnp.float32),
    )
    key_grad = (own_key + sibling_key[0, rows:] + earlier_key).astype(jnp.bfloat16)[None]
    value_grad = (own_value + sibling_value[0, rows:] + earlier_value).astype(jnp.bfloat16)[None]
    return (query_total.astype(jnp.bfloat16)[None], key_grad, value_grad)


def solution(mesh):
    placed = (
        P("thinker", "seq", None),
        P("thinker", "seq", None),
        P("thinker", "seq", None),
        P("thinker", "seq", None),
        P("thinker", None, "seq"),
        P(None, ("thinker", "seq"), None),
        P(),
        P("thinker", None, "seq"),
    )
    return jax.shard_map(
        shards,
        mesh=mesh,
        in_specs=placed,
        out_specs=(P("thinker", "seq", None), P("thinker", "seq", None), P("thinker", "seq", None)),
        check_vma=False,
    )
```

profile of v0, /device:TPU:0, one launch (start us, length us, event | category | flops | bytes accessed | tf_op | source)
XLA Modules:
  0.0 450.8 jit_solution(13187898375791302462)
XLA Ops:
  12.0 2.0 reduce
  15.2 11.2 %all-to-all-start = ((bf16[128,2,1024]{2,1,0:T(2,128)(2,1)}), bf16[128,2,1024]{2,1,0:T(2,128)(2,1)S(1)}, u32[]{:S(2)}, u32[]{:S(2)}) async-start(bf16[128,2,1024]{2,1,0:T(2,128)(2,1)} %reshape.165), calls=%async_computation | async-start | bytes 1048576 | tf_op jit(solution)/shard_map/all_to_all | solution.py:71
  26.5 15.7 %all_gather.15 = bf16[4,128,512]{2,1,0:T(8,128)(2,1)S(1)} all-gather(bf16[1,128,512]{2,1,0:T(8,128)(2,1)S(1)} %copy-done.17), channel_id=1, replica_groups=mesh['thinker'=4,'seq'=32] {'thinker'}, dimensions={0}, use_global_device_ids=true | all-gather | bytes 655360 | tf_op jit(solution)/shard_map/all_gather | solution.py:136
  42.4 2.1 collective-permute-start.1
  44.6 12.8 %all_gather.14 = bf16[4,128,512]{2,1,0:T(8,128)(2,1)S(1)} all-gather(bf16[1,128,512]{2,1,0:T(8,128)(2,1)S(1)} %copy-done.18), channel_id=1, replica_groups=mesh['thinker'=4,'seq'=32] {'thinker'}, dimensions={0}, use_global_device_ids=true | all-gather | bytes 655360 | tf_op jit(solution)/shard_map/all_gather | solution.py:135
  57.6 3.7 collective-permute-start
  70.2 1.9 copy.156
  73.3 2.3 fusion.57
  78.8 2.3 fusion.65
  96.7 2.2 fusion.63
  104.4 3.3 fusion.36
  108.5 14.2 %all-gather.5.cloned.1.call-done = bf16[1,4096,512]{1,2,0:T(8,128)(2,1)} async-done(((bf16[1,128,512]{1,2,0:T(8,128)(2,1)}), bf16[1,4096,512]{1,2,0:T(8,128)(2,1)}) %all-gather.5.cloned.1.call-update) | async-done | bytes 4194320 | tf_op jit(solution)/shard_map/all_gather | solution.py:109
  122.7 2.2 broadcast.167.clone2
  124.9 2.3 broadcast.167.clone
  127.2 147.3 %while.20 = (s32[]{:T(128)}, f32[128,2048]{0,1:T(8,128)}, bf16[4096,512]{1,0:T(8,128)(2,1)}, bf16[4096,512]{1,0:T(8,128)(2,1)}, bf16[4096,512]{0,1:T(8,128)(2,1)...) while((s32[]{:T(128)}, f32[128,2048]{0,1:T(8,128)}, ...), condition=%wide.region_2.3_spmd.clone.clone.clone, body=%wide.region_1.2_spmd.clone.clone.clone.sunk | while | flops 1354434432 | bytes 44792396 | solution.py:127
  130.9 1.8 fusion.145
  132.7 2.8 fusion.147
  135.5 2.5 fusion.146
  139.3 2.6 fusion.148
  149.4 1.8 fusion.145
  151.2 2.8 fusion.147
  154.0 2.5 fusion.146
  157.8 2.6 fusion.148
  169.6 2.8 fusion.147
  172.4 2.5 fusion.146
  176.2 2.6 fusion.148
  186.2 1.8 fusion.145
  188.0 2.8 fusion.147
  190.8 2.5 fusion.146
  194.6 2.6 fusion.148
  204.6 1.8 fusion.145
  206.4 2.8 fusion.147
  209.2 2.5 fusion.146
  213.0 2.6 fusion.148
  224.8 2.8 fusion.147
  227.6 2.5 fusion.146
  231.4 2.6 fusion.148
  241.3 1.8 fusion.145
  243.1 2.8 fusion.147
  246.0 2.5 fusion.146
  249.8 2.6 fusion.148
  259.7 1.8 fusion.145
  261.5 2.8 fusion.147
  264.4 2.5 fusion.146
  268.2 2.6 fusion.148
  287.9 2.7 fusion.69
  290.6 65.7 %reduce-scatter.9.cloned.1.call-done = bf16[128,512]{1,0:T(8,128)(2,1)} async-done(((bf16[4096,512]{1,0:T(8,128)(2,1)}), bf16[128,512]{1,0:T(8,128)(2,1)}) %reduce-scatter.9.cloned.1.call-update) | async-done | bytes 131088 | tf_op jit(solution)/shard_map/reduce_scatter | solution.py:132
  358.0 83.6 %reduce-scatter.5.cloned.1.call-done = bf16[128,512]{1,0:T(8,128)(2,1)} async-done(((bf16[4096,512]{1,0:T(8,128)(2,1)}), bf16[128,512]{1,0:T(8,128)(2,1)}) %reduce-scatter.5.cloned.1.call-update) | async-done | bytes 131088 | tf_op jit(solution)/shard_map/reduce_scatter | solution.py:131
  (261 shorter events, 127.1 us)
Async XLA Ops:
  8.0 18.5 %copy-start.17 = (bf16[1,128,512]{2,1,0:T(8,128)(2,1)S(1)}, bf16[1,128,512]{2,1,0:T(8,128)(2,1)}, u32[]{:S(2)}) copy-start(bf16[1,128,512]{2,1,0:T(8,128)(2,1)} %param.16) | copy-start | bytes 393220
  8.0 100.5 %all-gather.3.cloned.1.call-start = ((), (), s32[]{:S(2)}) async-start(), calls=%async_computation.5 | async-start | bytes 4325376 | tf_op jit(solution)/shard_map/all_gather | solution.py:108
  9.8 113.0 %all-gather.5.cloned.1.call-start = ((), (), s32[]{:S(2)}) async-start(), calls=%async_computation.6 | async-start | bytes 4325376 | tf_op jit(solution)/shard_map/all_gather | solution.py:109
  14.0 30.5 %copy-start.18 = (bf16[1,128,512]{2,1,0:T(8,128)(2,1)S(1)}, bf16[1,128,512]{2,1,0:T(8,128)(2,1)}, u32[]{:S(2)}) copy-start(bf16[1,128,512]{2,1,0:T(8,128)(2,1)} %param.15) | copy-start | bytes 393220
  15.2 46.2 %copy-start.22 = (s32[4]{0:T(128)S(1)}, s32[4]{0:T(128)}, u32[]{:S(2)}) copy-start(s32[4]{0:T(128)} %param.20) | copy-start | bytes 52
  15.2 46.8 %copy-start.23 = (s32[1,3,1]{1,2,0:T(1,128)S(1)}, s32[1,3,1]{1,2,0:T(1,128)}, u32[]{:S(2)}) copy-start(s32[1,3,1]{1,2,0:T(1,128)} %param.21) | copy-start | bytes 40
  15.2 50.7 %copy-start.19 = (bf16[1,128,2048]{2,1,0:T(8,128)(2,1)S(1)}, bf16[1,128,2048]{2,1,0:T(8,128)(2,1)}, u32[]{:S(2)}) copy-start(bf16[1,128,2048]{2,1,0:T(8,128)(2,1)} %param.14) | copy-start | bytes 1572868
  15.2 54.5 %all-to-all-start = ((bf16[128,2,1024]{2,1,0:T(2,128)(2,1)}), bf16[128,2,1024]{2,1,0:T(2,128)(2,1)S(1)}, u32[]{:S(2)}, u32[]{:S(2)}) async-start(bf16[128,2,1024]{2,1,0:T(2,128)(2,1)} %reshape.165), calls=%async_computation | async-start | bytes 1048576 | tf_op jit(solution)/shard_map/all_to_all | solution.py:71
  26.4 255.5 %reduce-scatter.11.cloned.1.call-start = ((), (), s32[]{:S(2)}) async-start(), calls=%async_computation.10 | async-start | bytes 1310720 | tf_op jit(solution)/shard_map/reduce_scatter | solution.py:176
  42.4 30.8 %collective-permute-start.1 = (bf16[4,128,512]{1,2,0:T(8,128)(2,1)S(1)}, bf16[4,128,512]{1,2,0:T(8,128)(2,1)}, u32[]{:S(2)}, u32[]{:S(2)}) collective-permute-start(bf16[4,128,512]{1,2,0:T(8,128)(2,1)S(1)} %copy.162), channel_id=1, source_target_pairs={{0,1},{1,2},{2,3},{3,4},{4,5},{5,6},{6,7},{7,8},{8,9},{9,10},{10,1... | collective-permute-start | bytes 1572872 | tf_op jit(solution)/shard_map/ppermute | solution.py:13
  57.6 15.6 %collective-permute-start = (bf16[4,128,512]{1,2,0:T(8,128)(2,1)S(1)}, bf16[4,128,512]{1,2,0:T(8,128)(2,1)}, u32[]{:S(2)}, u32[]{:S(2)}) collective-permute-start(bf16[4,128,512]{1,2,0:T(8,128)(2,1)S(1)} %copy.158), channel_id=1, source_target_pairs={{0,1},{1,2},{2,3},{3,4},{4,5},{5,6},{6,7},{7,8},{8,9},{9,10},{10,1... | collective-permute-start | bytes 1572872 | tf_op jit(solution)/shard_map/ppermute | solution.py:13
  73.2 3.9 copy-start.24
  84.6 1.0 copy-start.4
  85.6 1.7 copy-start.13
  89.0 1.7 copy-start.16
  107.7 176.6 %reduce-scatter.7.cloned.1.call-start = ((), (), s32[]{:S(2)}) async-start(), calls=%async_computation.8 | async-start | bytes 1310720 | tf_op jit(solution)/shard_map/reduce_scatter | solution.py:173
  108.2 248.1 %reduce-scatter.9.cloned.1.call-start = ((), (), s32[]{:S(2)}) async-start(), calls=%async_computation.9 | async-start | bytes 4325376 | tf_op jit(solution)/shard_map/reduce_scatter | solution.py:132
  142.0 1.3 copy-start
  143.3 1.2 copy-start.3
  143.5 1.0 copy-start.1
  160.5 1.2 copy-start
  161.7 1.2 copy-start.3
  161.9 1.0 copy-start.1
  178.9 1.2 copy-start
  180.1 1.2 copy-start.3
  197.2 1.2 copy-start
  198.5 1.2 copy-start.3
  215.6 1.2 copy-start
  216.9 1.2 copy-start.3
  234.0 1.2 copy-start
  235.2 1.2 copy-start.3
  252.4 1.2 copy-start
  253.6 1.2 copy-start.3
  270.8 1.2 copy-start
  272.0 1.2 copy-start.3
  274.6 166.9 %reduce-scatter.5.cloned.1.call-start = ((), (), s32[]{:S(2)}) async-start(), calls=%async_computation.7 | async-start | bytes 4325376 | tf_op jit(solution)/shard_map/reduce_scatter | solution.py:131
  274.7 1.2 copy-start.5
  274.7 1.3 copy-start.15
  275.9 1.7 copy-start.7
  277.6 2.7 copy-start.9
  277.6 2.7 copy-start.12
  280.3 6.2 %copy-start.2 = (f32[128,2048]{0,1:T(8,128)S(1)}, f32[128,2048]{0,1:T(8,128)}, u32[]{:S(2)}) copy-start(f32[128,2048]{0,1:T(8,128)} %get-tuple-element.221) | copy-start | bytes 3145732
  280.6 7.2 %copy-start.10 = (f32[128,2048]{1,0:T(8,128)S(1)}, f32[128,2048]{1,0:T(8,128)}, u32[]{:S(2)}) copy-start(f32[128,2048]{1,0:T(8,128)} %copy.174) | copy-start | bytes 3145732
  282.0 5.9 %copy-start.11 = (f32[128,2048]{1,0:T(8,128)S(1)}, f32[128,2048]{1,0:T(8,128)}, u32[]{:S(2)}) copy-start(f32[128,2048]{1,0:T(8,128)} %copy.168) | copy-start | bytes 3145732
  283.0 7.6 %collective-permute-start.3 = (bf16[128,512]{1,0:T(8,128)(2,1)S(1)}, bf16[128,512]{1,0:T(8,128)(2,1)}, u32[]{:S(2)}, u32[]{:S(2)}) collective-permute-start(bf16[128,512]{1,0:T(8,128)(2,1)S(1)} %slice_bitcast_fusion), channel_id=1, source_target_pairs={{1,0},{2,1},{3,2},{4,3},{5,4},{6,5},{7,6},{8,7},{9,8},{10,9},{11,1... | collective-permute-start | bytes 393224 | tf_op jit(solution)/shard_map/ppermute | solution.py:13
  285.2 72.8 %collective-permute-start.2 = (bf16[128,512]{1,0:T(8,128)(2,1)S(1)}, bf16[128,512]{1,0:T(8,128)(2,1)S(1)}, u32[]{:S(2)}, u32[]{:S(2)}) collective-permute-start(bf16[128,512]{1,0:T(8,128)(2,1)S(1)} %slice_bitcast_fusion.2), channel_id=1, source_target_pairs={{1,0},{2,1},{3,2},{4,3},{5,4},{6,5},{7,6},{8,7},{9,8},{10,9},{11,1... | collective-permute-start | bytes 393224 | tf_op jit(solution)/shard_map/ppermute | solution.py:13
  287.9 68.5 %copy-start.20 = (bf16[1,256,512]{2,1,0:T(8,128)(2,1)S(1)}, bf16[1,256,512]{2,1,0:T(8,128)(2,1)}, u32[]{:S(2)}) copy-start(bf16[1,256,512]{2,1,0:T(8,128)(2,1)} %reduce-scatter.11.cloned.1.call-done) | copy-start | bytes 786436
  287.9 153.7 %copy-start.21 = (bf16[1,256,512]{2,1,0:T(8,128)(2,1)S(1)}, bf16[1,256,512]{2,1,0:T(8,128)(2,1)}, u32[]{:S(2)}) copy-start(bf16[1,256,512]{2,1,0:T(8,128)(2,1)} %reduce-scatter.7.cloned.1.call-done) | copy-start | bytes 786436
  (9 other events, 8.7 us)
Sparse Core Ops, SparseCore 0:
  11.6 57.4 all-gather.2
  71.8 50.8 all-gather.4
Sparse Core Ops, SparseCore 1:
  107.7 24.0 reduce-scatter.10
  134.1 23.7 reduce-scatter.6
  274.7 81.6 reduce-scatter.8
  360.0 81.5 reduce-scatter.4
where the time goes:
time: 455 us; the launch traced here: 451 us
  waiting for transfers between devices  165 us (36%)
  matrix products  104 us (23%)
  local copies, waits for them, and re-layouts  83.9 us (18%)
  other arithmetic  30.5 us (7%)
  blocking collectives  28.5 us (6%)
  starting transfers between devices  20.1 us (4%)
  between operations  18.1 us (4%)
    reduce_scatter x1, waiting for transfers between devices, shards(): lax.psum_scatter(key_buffer, 'seq', scatter_dimension=0, tiled=True)  83.6 us
    reduce_scatter x1, waiting for transfers between devices, shards(): lax.psum_scatter(value_buffer, 'seq', scatter_dimension=0, tiled=True)  65.7 us
    dot_general x11, matrix products, pair_grads(): jnp.einsum('kgij,ikgd->jkd', probs_low, upstream_heads, preferred_element...  28.6 us
    dot_general x11, matrix products, pair_grads(): jnp.einsum('kgij,ikgd->jkd', dscores_low, query_heads, preferred_element_...  25.7 us
    dot_general x11, matrix products, pair_grads(): jnp.einsum('ikgd,jkd->kgij', upstream_heads, value_heads, preferred_eleme...  25 us
    dot_general x11, matrix products, pair_grads(): jnp.einsum('ikgd,jkd->kgij', query_heads, key_heads, preferred_element_ty...  19.4 us
    dynamic_update_slice x16, local copies, waits for them, and re-layouts, one_block(): lax.dynamic_update_slice_in_dim(value_buffer, value_part.astype(jnp.bfloa...  18.4 us
    all_gather x1, blocking collectives, shards(): lax.all_gather(values, 'thinker', axis=0, tiled=True)  15.7 us
  transfers between devices with their start and end apart: 11, of which 3 were waited for; matrix products, arithmetic and copies ran while one was open for 44% of the time, Pallas kernels for 0%

commit v1 on v0

--- a/solution.py
+++ b/solution.py
@@ -52,6 +52,12 @@
 
 
 def shards(queries, keys, values, forward_out, logsumexp, upstream, lengths, sibling_mask):
+
+    def recover_slot_on_mesh(body):
+        row_out = jnp.stack([body for _ in range(lax.axis_size("thinker"))], axis=0)
+        carry_out = jnp.concatenate(lax.all_to_all(row_out, "thinker", 0, 0), 0)
+        return carry_out
+
     thinkers = lax.axis_size("thinker")
     seq_count = lax.axis_size("seq")
     devices = thinkers * seq_count
@@ -133,7 +139,7 @@
     )
     sibling_keys, sibling_values = (
         lax.all_gather(keys, "thinker", axis=0, tiled=True),
-        lax.all_gather(values, "thinker", axis=0, tiled=True),
+        recover_slot_on_mesh(values),
     )
     prior_keys, prior_values = from_behind((sibling_keys, sibling_values), "seq", 1)
     window_keys = jnp.roll(jnp.concatenate([prior_keys, sibling_keys], axis=1), -thinker, axis=0)

time: 455 us -> 456 us (level)
  blocking collectives: 28.5 us -> 17.8 us
  waiting for transfers between devices: 165 us -> 173 us
    all_gather x1 -> x0, blocking collectives: 15.7 us -> none  [shards(): lax.all_gather(values, 'thinker', axis=0, tiled=True)]
    all_to_all x1, waiting for transfers between devices: 0.01 us -> 6.22 us  [shards(): lax.all_to_all(arranged, ('thinker', 'seq'), split_axis=0, concat_axis=2,...]
    all_to_all x0 -> x1, starting transfers between devices: none -> 5.42 us  [recover_slot_on_mesh(): carry_out = jnp.concatenate(lax.all_to_all(row_out, 'thinker', 0, 0), 0)]
    all_gather x1, blocking collectives: 12.8 us -> 17.8 us  [shards(): lax.all_gather(keys, 'thinker', axis=0, tiled=True)]
  transfers between devices with their start and end apart: 11 -> 12, of which waited for: 3 -> 4; matrix products, arithmetic and copies ran while one was open for 44% -> 44% of each run, Pallas kernels for 0% -> 0%
where the time goes in v1:
time: 456 us; the launch traced here: 452 us
  waiting for transfers between devices  173 us (38%)
  matrix products  104 us (23%)
  local copies, waits for them, and re-layouts  85.4 us (19%)
  other arithmetic  30.9 us (7%)
  starting transfers between devices  22 us (5%)
  between operations  18.1 us (4%)
  blocking collectives  17.8 us (4%)
    reduce_scatter x1, waiting for transfers between devices, shards(): lax.psum_scatter(key_buffer, 'seq', scatter_dimension=0, tiled=True)  83.6 us
    reduce_scatter x1, waiting for transfers between devices, shards(): lax.psum_scatter(value_buffer, 'seq', scatter_dimension=0, tiled=True)  65.9 us
    dot_general x11, matrix products, pair_grads(): jnp.einsum('kgij,ikgd->jkd', probs_low, upstream_heads, preferred_element...  28.6 us
    dot_general x11, matrix products, pair_grads(): jnp.einsum('kgij,ikgd->jkd', dscores_low, query_heads, preferred_element_...  25.8 us
    dot_general x11, matrix products, pair_grads(): jnp.einsum('ikgd,jkd->kgij', upstream_heads, value_heads, preferred_eleme...  25 us
    dot_general x11, matrix products, pair_grads(): jnp.einsum('ikgd,jkd->kgij', query_heads, key_heads, preferred_element_ty...  19.4 us
    dynamic_update_slice x16, local copies, waits for them, and re-layouts, one_block(): lax.dynamic_update_slice_in_dim(value_buffer, value_part.astype(jnp.bfloa...  18.4 us
    all_gather x1, blocking collectives, shards(): lax.all_gather(keys, 'thinker', axis=0, tiled=True)  17.8 us
  transfers between devices with their start and end apart: 12, of which 4 were waited for; matrix products, arithmetic and copies ran while one was open for 44% of the time, Pallas kernels for 0%

profile of v1, /device:TPU:0, one launch (start us, length us, event | category | flops | bytes accessed | tf_op | source)
XLA Modules:
  0.0 451.9 jit_solution(16360508699661933878)
XLA Ops:
  13.5 5.4 %all-to-all-start.1 = ((bf16[4,1,128,512]{2,3,1,0:T(8,128)(2,1)}), bf16[4,1,128,512]{2,3,1,0:T(8,128)(2,1)S(1)}, u32[]{:S(2)}, u32[]{:S(2)}) async-start(bf16[4,1,128,512]{2,3,1,0:T(8,128)(2,1)} %stack.6), calls=%async_computation.1 | async-start | bytes 1048576 | tf_op jit(solution)/shard_map/all_to_all | solution.py:58
  18.9 17.8 %all_gather.11 = bf16[4,128,512]{2,1,0:T(8,128)(2,1)S(1)} all-gather(bf16[1,128,512]{2,1,0:T(8,128)(2,1)S(1)} %copy-done.17), channel_id=1, replica_groups=mesh['thinker'=4,'seq'=32] {'thinker'}, dimensions={0}, use_global_device_ids=true | all-gather | bytes 655360 | tf_op jit(solution)/shard_map/all_gather | solution.py:141
  37.0 2.1 collective-permute-start
  43.2 9.2 %all-to-all-start = ((bf16[128,2,1024]{2,1,0:T(2,128)(2,1)}), bf16[128,2,1024]{2,1,0:T(2,128)(2,1)S(1)}, u32[]{:S(2)}, u32[]{:S(2)}) async-start(bf16[128,2,1024]{2,1,0:T(2,128)(2,1)} %reshape.172), calls=%async_computation | async-start | bytes 1048576 | tf_op jit(solution)/shard_map/all_to_all | solution.py:77
  53.1 2.2 collective-permute-start.1
  61.7 6.2 %all-to-all-done = bf16[128,2,1024]{2,1,0:T(2,128)(2,1)S(1)} async-done(((bf16[128,2,1024]{2,1,0:T(2,128)(2,1)}), bf16[128,2,1024]{2,1,0:T(2,128)(2,1)S(1)}, u32[]{:S(2)}, u32[]{:S(2)}) %all-to-all-start) | async-done | bytes 524320 | tf_op jit(solution)/shard_map/all_to_all | solution.py:77
  68.3 1.9 copy.155
  71.5 2.3 fusion.57
  77.0 2.2 fusion.65
  94.9 2.2 fusion.63
  102.5 3.3 fusion.36
  106.6 15.9 %all-gather.5.cloned.1.call-done = bf16[1,4096,512]{1,2,0:T(8,128)(2,1)} async-done(((bf16[1,128,512]{1,2,0:T(8,128)(2,1)}), bf16[1,4096,512]{1,2,0:T(8,128)(2,1)}) %all-gather.5.cloned.1.call-update) | async-done | bytes 4194320 | tf_op jit(solution)/shard_map/all_gather | solution.py:115
  122.6 2.2 broadcast.170.clone2
  124.8 2.3 broadcast.170.clone
  127.1 148.5 %while.20 = (s32[]{:T(128)}, f32[128,2048]{0,1:T(8,128)}, bf16[4096,512]{1,0:T(8,128)(2,1)}, bf16[4096,512]{1,0:T(8,128)(2,1)}, bf16[4096,512]{0,1:T(8,128)(2,1)...) while((s32[]{:T(128)}, f32[128,2048]{0,1:T(8,128)}, ...), condition=%wide.region_2.3_spmd.clone.clone.clone, body=%wide.region_1.2_spmd.clone.clone.clone.sunk | while | flops 1354434432 | bytes 44792396 | solution.py:133
  130.9 1.8 fusion.145
  132.7 2.8 fusion.147
  135.5 2.5 fusion.146
  139.3 2.6 fusion.148
  151.3 2.8 fusion.147
  154.1 2.5 fusion.146
  157.9 2.6 fusion.148
  168.0 1.8 fusion.145
  169.8 2.8 fusion.147
  172.6 2.5 fusion.146
  176.4 2.6 fusion.148
  186.5 1.8 fusion.145
  188.3 2.8 fusion.147
  191.2 2.5 fusion.146
  195.0 2.6 fusion.148
  205.1 1.8 fusion.145
  206.9 2.8 fusion.147
  209.7 2.5 fusion.146
  213.5 2.6 fusion.148
  223.6 1.8 fusion.145
  225.4 2.8 fusion.147
  228.2 2.5 fusion.146
  232.1 2.6 fusion.148
  242.2 1.8 fusion.145
  244.0 2.8 fusion.147
  246.8 2.5 fusion.146
  250.6 2.6 fusion.148
  262.5 2.8 fusion.147
  265.3 2.5 fusion.146
  269.1 2.6 fusion.148
  288.8 2.7 fusion.69
  291.5 65.9 %reduce-scatter.9.cloned.1.call-done = bf16[128,512]{1,0:T(8,128)(2,1)} async-done(((bf16[4096,512]{1,0:T(8,128)(2,1)}), bf16[128,512]{1,0:T(8,128)(2,1)}) %reduce-scatter.9.cloned.1.call-update) | async-done | bytes 131088 | tf_op jit(solution)/shard_map/reduce_scatter | solution.py:138
  359.1 83.6 %reduce-scatter.5.cloned.1.call-done = bf16[128,512]{1,0:T(8,128)(2,1)} async-done(((bf16[4096,512]{1,0:T(8,128)(2,1)}), bf16[128,512]{1,0:T(8,128)(2,1)}) %reduce-scatter.5.cloned.1.call-update) | async-done | bytes 131088 | tf_op jit(solution)/shard_map/reduce_scatter | solution.py:137
  (263 shorter events, 131.0 us)
Async XLA Ops:
  8.0 10.9 %copy-start.17 = (bf16[1,128,512]{2,1,0:T(8,128)(2,1)S(1)}, bf16[1,128,512]{2,1,0:T(8,128)(2,1)}, u32[]{:S(2)}) copy-start(bf16[1,128,512]{2,1,0:T(8,128)(2,1)} %param.15) | copy-start | bytes 393220
  8.0 98.6 %all-gather.3.cloned.1.call-start = ((), (), s32[]{:S(2)}) async-start(), calls=%async_computation.6 | async-start | bytes 4325376 | tf_op jit(solution)/shard_map/all_gather | solution.py:114
  9.8 29.9 %copy-start.19 = (bf16[128,1,2048]{2,0,1:T(8,128)(2,1)S(1)}, bf16[128,1,2048]{2,0,1:T(8,128)(2,1)}, u32[]{:S(2)}) copy-start(bf16[128,1,2048]{2,0,1:T(8,128)(2,1)} %param.19) | copy-start | bytes 1572868
  9.8 112.8 %all-gather.5.cloned.1.call-start = ((), (), s32[]{:S(2)}) async-start(), calls=%async_computation.7 | async-start | bytes 4325376 | tf_op jit(solution)/shard_map/all_gather | solution.py:115
  13.5 29.7 %all-to-all-start.1 = ((bf16[4,1,128,512]{2,3,1,0:T(8,128)(2,1)}), bf16[4,1,128,512]{2,3,1,0:T(8,128)(2,1)S(1)}, u32[]{:S(2)}, u32[]{:S(2)}) async-start(bf16[4,1,128,512]{2,3,1,0:T(8,128)(2,1)} %stack.6), calls=%async_computation.1 | async-start | bytes 1048576 | tf_op jit(solution)/shard_map/all_to_all | solution.py:58
  18.9 23.0 %copy-start.22 = (s32[4]{0:T(128)S(1)}, s32[4]{0:T(128)}, u32[]{:S(2)}) copy-start(s32[4]{0:T(128)} %param.20) | copy-start | bytes 52
  18.9 23.6 %copy-start.23 = (s32[1,3,1]{1,2,0:T(1,128)S(1)}, s32[1,3,1]{1,2,0:T(1,128)}, u32[]{:S(2)}) copy-start(s32[1,3,1]{1,2,0:T(1,128)} %param.21) | copy-start | bytes 40
  36.7 21.2 %copy-start.18 = (bf16[1,128,2048]{2,1,0:T(8,128)(2,1)S(1)}, bf16[1,128,2048]{2,1,0:T(8,128)(2,1)}, u32[]{:S(2)}) copy-start(bf16[1,128,2048]{2,1,0:T(8,128)(2,1)} %param.14) | copy-start | bytes 1572868
  37.0 34.4 %collective-permute-start = (bf16[4,128,512]{1,2,0:T(8,128)(2,1)S(1)}, bf16[4,128,512]{1,2,0:T(8,128)(2,1)}, u32[]{:S(2)}, u32[]{:S(2)}) collective-permute-start(bf16[4,128,512]{1,2,0:T(8,128)(2,1)S(1)} %copy.157), channel_id=1, source_target_pairs={{0,1},{1,2},{2,3},{3,4},{4,5},{5,6},{6,7},{7,8},{8,9},{9,10},{10,1... | collective-permute-start | bytes 1572872 | tf_op jit(solution)/shard_map/ppermute | solution.py:13
  43.2 24.7 %all-to-all-start = ((bf16[128,2,1024]{2,1,0:T(2,128)(2,1)}), bf16[128,2,1024]{2,1,0:T(2,128)(2,1)S(1)}, u32[]{:S(2)}, u32[]{:S(2)}) async-start(bf16[128,2,1024]{2,1,0:T(2,128)(2,1)} %reshape.172), calls=%async_computation | async-start | bytes 1048576 | tf_op jit(solution)/shard_map/all_to_all | solution.py:77
  52.4 230.5 %reduce-scatter.11.cloned.1.call-start = ((), (), s32[]{:S(2)}) async-start(), calls=%async_computation.11 | async-start | bytes 1310720 | tf_op jit(solution)/shard_map/reduce_scatter | solution.py:182
  53.1 18.3 %collective-permute-start.1 = (bf16[4,128,512]{1,2,0:T(8,128)(2,1)S(1)}, bf16[4,128,512]{1,2,0:T(8,128)(2,1)}, u32[]{:S(2)}, u32[]{:S(2)}) collective-permute-start(bf16[4,128,512]{1,2,0:T(8,128)(2,1)S(1)} %bitcast.305), channel_id=1, source_target_pairs={{0,1},{1,2},{2,3},{3,4},{4,5},{5,6},{6,7},{7,8},{8,9},{9,10},{10,1... | collective-permute-start | bytes 1572872 | tf_op jit(solution)/shard_map/ppermute | solution.py:13
  71.4 3.9 copy-start.24
  82.8 1.0 copy-start.4
  83.8 1.7 copy-start.13
  87.2 1.7 copy-start.16
  105.8 179.4 %reduce-scatter.7.cloned.1.call-start = ((), (), s32[]{:S(2)}) async-start(), calls=%async_computation.9 | async-start | bytes 1310720 | tf_op jit(solution)/shard_map/reduce_scatter | solution.py:179
  106.4 251.0 %reduce-scatter.9.cloned.1.call-start = ((), (), s32[]{:S(2)}) async-start(), calls=%async_computation.10 | async-start | bytes 4325376 | tf_op jit(solution)/shard_map/reduce_scatter | solution.py:138
  141.9 1.2 copy-start
  143.2 1.2 copy-start.3
  160.5 1.2 copy-start
  161.8 1.2 copy-start.3
  179.1 1.2 copy-start
  180.3 1.2 copy-start.3
  180.5 1.0 copy-start.1
  197.6 1.2 copy-start
  198.8 1.2 copy-start.3
  216.2 1.2 copy-start
  217.4 1.2 copy-start.3
  234.7 1.2 copy-start
  235.9 1.2 copy-start.3
  253.2 1.2 copy-start
  254.5 1.2 copy-start.3
  271.8 1.2 copy-start
  273.0 1.2 copy-start.3
  275.5 167.1 %reduce-scatter.5.cloned.1.call-start = ((), (), s32[]{:S(2)}) async-start(), calls=%async_computation.8 | async-start | bytes 4325376 | tf_op jit(solution)/shard_map/reduce_scatter | solution.py:137
  275.6 1.2 copy-start.5
  275.6 1.3 copy-start.15
  276.9 1.7 copy-start.7
  278.5 2.7 copy-start.9
  278.5 2.7 copy-start.12
  281.2 6.2 %copy-start.2 = (f32[128,2048]{0,1:T(8,128)S(1)}, f32[128,2048]{0,1:T(8,128)}, u32[]{:S(2)}) copy-start(f32[128,2048]{0,1:T(8,128)} %get-tuple-element.221) | copy-start | bytes 3145732
  281.5 7.2 %copy-start.10 = (f32[128,2048]{1,0:T(8,128)S(1)}, f32[128,2048]{1,0:T(8,128)}, u32[]{:S(2)}) copy-start(f32[128,2048]{1,0:T(8,128)} %copy.172) | copy-start | bytes 3145732
  282.9 5.9 %copy-start.11 = (f32[128,2048]{1,0:T(8,128)S(1)}, f32[128,2048]{1,0:T(8,128)}, u32[]{:S(2)}) copy-start(f32[128,2048]{1,0:T(8,128)} %copy.166) | copy-start | bytes 3145732
  283.9 7.6 %collective-permute-start.3 = (bf16[128,512]{1,0:T(8,128)(2,1)S(1)}, bf16[128,512]{1,0:T(8,128)(2,1)}, u32[]{:S(2)}, u32[]{:S(2)}) collective-permute-start(bf16[128,512]{1,0:T(8,128)(2,1)S(1)} %slice_bitcast_fusion), channel_id=1, source_target_pairs={{1,0},{2,1},{3,2},{4,3},{5,4},{6,5},{7,6},{8,7},{9,8},{10,9},{11,1... | collective-permute-start | bytes 393224 | tf_op jit(solution)/shard_map/ppermute | solution.py:13
  286.1 72.9 %collective-permute-start.2 = (bf16[128,512]{1,0:T(8,128)(2,1)S(1)}, bf16[128,512]{1,0:T(8,128)(2,1)S(1)}, u32[]{:S(2)}, u32[]{:S(2)}) collective-permute-start(bf16[128,512]{1,0:T(8,128)(2,1)S(1)} %slice_bitcast_fusion.2), channel_id=1, source_target_pairs={{1,0},{2,1},{3,2},{4,3},{5,4},{6,5},{7,6},{8,7},{9,8},{10,9},{11,1... | collective-permute-start | bytes 393224 | tf_op jit(solution)/shard_map/ppermute | solution.py:13
  288.8 68.6 %copy-start.20 = (bf16[1,256,512]{2,1,0:T(8,128)(2,1)S(1)}, bf16[1,256,512]{2,1,0:T(8,128)(2,1)}, u32[]{:S(2)}) copy-start(bf16[1,256,512]{2,1,0:T(8,128)(2,1)} %reduce-scatter.11.cloned.1.call-done) | copy-start | bytes 786436
  288.8 153.9 %copy-start.21 = (bf16[1,256,512]{2,1,0:T(8,128)(2,1)S(1)}, bf16[1,256,512]{2,1,0:T(8,128)(2,1)}, u32[]{:S(2)}) copy-start(bf16[1,256,512]{2,1,0:T(8,128)(2,1)} %reduce-scatter.7.cloned.1.call-done) | copy-start | bytes 786436
  (10 other events, 9.6 us)
Sparse Core Ops, SparseCore 0:
  11.6 59.9 all-gather.2
  74.3 48.2 all-gather.4
Sparse Core Ops, SparseCore 1:
  105.9 22.0 reduce-scatter.10
  130.2 23.4 reduce-scatter.6
  275.6 81.7 reduce-scatter.8
  361.1 81.5 reduce-scatter.4
